TPU v7x, 32 devices: a whole 2x2x4 slice. The times are simulated.
32 devices in a mesh: grp: 2 (over core), dom: 8 (over z, x), sub: 2 (over y).
Axes of the slice: x: 2, y: 2, z: 4, core: 2. Of those that a mesh axis runs over, the one named last changes fastest.
Arguments:
- positions: float32 [3, 8192], P(None, ('grp', 'dom', 'sub')), may hold values from 0 to 4
- charges: float32 [8192], P(('grp', 'dom', 'sub')), may hold values from -3 to 3
- polar: float32 [8192], P(('grp', 'dom', 'sub')), may hold values from 0.1 to 0.6
- features: bfloat16 [8192, 256], P(('grp', 'dom', 'sub')), may hold values from -6 to 6
- neighbours: int32 [8192, 32], P(('grp', 'dom', 'sub')), may hold values from 0 to 512, as said below
- send_rows: int32 [2, 4096], P(None, ('grp', 'dom', 'sub')), may hold values from 0 to 255
- blocks: int32 [128], P(('grp', 'dom', 'sub')), may hold values from 0 to 31
- radial_in: bfloat16 [2, 8, 64], replicated, may hold values from -2 to 2
- radial_mid: bfloat16 [2, 2, 64, 64], replicated, may hold values from -0.75 to 0.75
- radial_out: bfloat16 [2, 64, 256], replicated, may hold values from -0.75 to 0.75
- node_in: bfloat16 [2, 256, 256], replicated, may hold values from -0.375 to 0.375
- node_out: bfloat16 [2, 256, 256], replicated, may hold values from -0.375 to 0.375
- field_gain: float32 [256], replicated, may hold values from -3 to 3
- readout: bfloat16 [256, 2], replicated, may hold values from -0.375 to 0.375
Outputs:
- site_result: float32 [3, 8192], P(None, ('grp', 'dom', 'sub'))
- response: float32 [3, 8192], P(None, ('grp', 'dom', 'sub'))
Inputs may be any that keep to these rules, and one draw needn't show every extreme that they name: `neighbours`: entries below 256 name the block's own sites, entries from 256 to 511 its lent sites, 512 an empty slot; empty slots follow the used ones. `blocks`: repeats may occur.
All inputs are finite; a program needn't handle non-finite values.
Results may differ from a plain program's by a relative error of at most 0.0022.
The roundings to bfloat16 on the way count: a program that leaves them out, or rounds other values in their place, can miss the bound.
Values may be sent and summed in bfloat16 or wider, within the bound.
A program may use at most 64 MiB of HBM per device.

v0:
```python
import jax
import jax.numpy as jnp
from jax import lax
from jax.sharding import PartitionSpec as P

BASIS = 8
LAYERS = 2
SWEEPS = 4
BLOCK = 128


SMOOTH = 1.0
GAMMA = 1.0
SPACING = 0.75


def with_halo(block, sides, width):
    for axis, dim in sides:
        count = lax.axis_size(axis)
        forward = [(i, i + 1) for i in range(count - 1)]
        backward = [(target, source) for source, target in forward]
        low = lax.ppermute(
            lax.slice_in_dim(block, block.shape[dim] - width, None, axis=dim), axis, forward
        )
        high = lax.ppermute(lax.slice_in_dim(block, 0, width, axis=dim), axis, backward)
        block = jnp.concatenate([low, block, high], axis=dim)
    return block


def partner_2(value, axis, bit):
    mask = 2**bit
    pairs = [(source, source ^ mask) for source in range(lax.axis_size(axis))]
    return lax.ppermute(value, axis, pairs)


def field_at(target, source, charge, dipole):
    tile_count = target.shape[1] // BLOCK
    tiles = target.reshape(3, tile_count, BLOCK).transpose(1, 0, 2)

    def field_one_tile(target_tile):
        offset = target_tile[:, :, None] - source[:, None, :]
        dist_sq = jnp.sum(offset * offset, axis=0) + SMOOTH
        inverse = lax.rsqrt(dist_sq)
        inverse_cube = inverse * inverse * inverse
        inverse_fifth = inverse_cube * inverse * inverse
        projected = jnp.sum(offset * dipole[:, None, :], axis=0)
        source_scale = charge[None, :] * inverse_cube + 3.0 * projected * inverse_fifth
        return jnp.sum(
            offset * source_scale[None] - dipole[:, None, :] * inverse_cube[None], axis=2
        )

    return lax.map(field_one_tile, tiles).transpose(1, 0, 2).reshape(3, -1)


def slot_field(offset, dist_sq, source_charge, source_dipole):
    inverse = lax.rsqrt(dist_sq)
    inverse_cube = inverse * inverse * inverse
    inverse_fifth = inverse_cube * inverse * inverse
    projected = jnp.sum(offset * source_dipole, axis=0)
    source_scale = source_charge * inverse_cube + 3.0 * projected * inverse_fifth
    return jnp.sum(offset * source_scale[None] - source_dipole * inverse_cube[None], axis=1)


def message_update(
    hidden, lifted_table, radial_basis, slot_major, w_first, w_middle, w_last, w_node
):
    row_count, channel_count = hidden.shape
    slot_count = slot_major.shape[0]
    basis_width = radial_basis.shape[2]
    tile_count = row_count // BLOCK

    def message_one_tile(tile_index):
        start = tile_index * BLOCK
        basis_tile = lax.dynamic_slice_in_dim(radial_basis, start, BLOCK, 1).reshape(
            slot_count * BLOCK, basis_width
        )
        index_tile = lax.dynamic_slice_in_dim(slot_major, start, BLOCK, 1)
        first_hidden = jax.nn.silu(
            jnp.dot(basis_tile, w_first, preferred_element_type=jnp.float32)
        ).astype(jnp.bfloat16)
        second_hidden = jax.nn.silu(
            jnp.dot(first_hidden, w_middle[0], preferred_element_type=jnp.float32)
        ).astype(jnp.bfloat16)
        third_hidden = jax.nn.silu(
            jnp.dot(second_hidden, w_middle[1], preferred_element_type=jnp.float32)
        ).astype(jnp.bfloat16)
        edge_weight = jnp.dot(third_hidden, w_last, preferred_element_type=jnp.float32).reshape(
            slot_count, BLOCK, channel_count
        )
        source = lifted_table[index_tile].astype(jnp.float32)
        summed = jnp.sum(edge_weight * source, axis=0)
        return summed / slot_count

    message = (
        lax.map(message_one_tile, jnp.arange(tile_count, dtype=jnp.int32))
        .reshape(row_count, channel_count)
        .astype(jnp.bfloat16)
    )
    update = jax.nn.silu(jnp.dot(message, w_node, preferred_element_type=jnp.float32))
    return (hidden.astype(jnp.float32) + update).astype(jnp.bfloat16)


def extend_cols(values, rim_rows, rim_width):
    empty_entry = jnp.zeros(values.shape[:-1] + (1,), values.dtype)
    return jnp.concatenate(
        [values, rim_rows[..., :rim_width], rim_rows[..., 3 * rim_width :], empty_entry], axis=-1
    )


def extend_rows(values, rim_rows, rim_width):
    empty_entry = jnp.zeros((1,) + values.shape[1:], values.dtype)
    return jnp.concatenate(
        [values, rim_rows[:rim_width], rim_rows[3 * rim_width :], empty_entry], axis=0
    )


def local(
    positions,
    charges,
    polar,
    features,
    neighbours,
    send_rows,
    blocks,
    radial_in,
    radial_mid,
    radial_out,
    node_in,
    node_out,
    field_gain,
    readout,
):
    rim_width = send_rows.shape[1]
    row_count = positions.shape[1]
    block_width = BLOCK
    own_blocks = row_count // block_width
    domain_index = lax.axis_index(("dom", "sub"))
    learned = lax.axis_index("grp") == 0
    slot_major = neighbours.T
    local_data = jnp.concatenate([positions, charges[None], polar[None]], axis=0)
    outgoing = jnp.concatenate([local_data[:, send_rows[1]], local_data[:, send_rows[0]]], axis=1)
    rim_rows = with_halo(outgoing, ((("dom", "sub"), 1),), rim_width)
    site_table = extend_cols(local_data, rim_rows, rim_width)
    partner = partner_2(local_data, "grp", 0)
    others = lax.all_gather(partner, ("dom", "sub"), axis=1, tiled=True)
    near_sites = jnp.take(others.reshape(5, -1, block_width), blocks, axis=1).reshape(5, -1)
    outside = field_at(positions, near_sites[:3], near_sites[3], jnp.zeros_like(near_sites[:3]))
    offset = positions[:, None, :] - site_table[:3][:, slot_major]
    dist_sq = jnp.sum(offset * offset, axis=0) + SMOOTH
    strength = jnp.sqrt(1.0 + jnp.sum(outside * outside, axis=0))
    hidden = (features.astype(jnp.float32) + strength[:, None] * field_gain[None, :]).astype(
        jnp.bfloat16
    )
    centres = jnp.arange(BASIS, dtype=jnp.float32) * SPACING
    radial_basis = jnp.exp(-GAMMA * (jnp.sqrt(dist_sq)[:, :, None] - centres) ** 2).astype(
        jnp.bfloat16
    )
    for layer_index in range(LAYERS):
        lifted = lax.cond(
            learned,
            lambda h: jnp.dot(h, node_in[layer_index], preferred_element_type=jnp.float32).astype(
                jnp.bfloat16
            ),
            lambda h: jnp.zeros_like(h),
            hidden,
        )
        lent = jnp.concatenate([lifted[send_rows[1]], lifted[send_rows[0]]], axis=0)
        lifted_rims = with_halo(lent, ((("dom", "sub"), 0),), rim_width)
        lifted_table = extend_rows(lifted, lifted_rims, rim_width)
        hidden = lax.cond(
            learned,
            lambda h, t: message_update(
                h,
                t,
                radial_basis,
                slot_major,
                radial_in[layer_index],
                radial_mid[layer_index],
                radial_out[layer_index],
                node_out[layer_index],
            ),
            lambda h, t: h,
            hidden,
            lifted_table,
        )
    readouts = jnp.dot(hidden, readout, preferred_element_type=jnp.float32)
    charge = readouts[:, 0]
    energy = readouts[:, 1]
    fixed_field = outside + slot_field(
        offset, dist_sq, site_table[3][slot_major], jnp.zeros_like(offset)
    )
    dipole = jnp.where(learned, 0.0, polar[None] * fixed_field)
    for sweep_index in range(SWEEPS):
        lent_dipoles = jnp.concatenate([dipole[:, send_rows[1]], dipole[:, send_rows[0]]], axis=1)
        dipole_rims = with_halo(lent_dipoles, ((("dom", "sub"), 1),), rim_width)
        dipole_table = extend_cols(dipole, dipole_rims, rim_width)
        dipole = lax.cond(
            learned,
            lambda d, t: d,
            lambda d, t: polar[None]
            * (
                fixed_field + slot_field(offset, dist_sq, jnp.zeros_like(dist_sq), t[:, slot_major])
            ),
            dipole,
            dipole_table,
        )
    site_result = jnp.where(learned, jnp.stack([charge, energy, strength]), dipole)
    source_charge = jnp.where(learned, charge, 0.0)
    source_dipole = jnp.where(learned, 0.0, dipole)
    response_term = field_at(near_sites[:3], positions, source_charge, source_dipole)
    tiles, tile_ids = (
        lax.all_gather(response_term, ("dom", "sub"), axis=1, tiled=True),
        lax.all_gather(blocks, ("dom", "sub"), axis=0, tiled=True),
    )
    mine = domain_index * own_blocks + lax.broadcasted_iota(jnp.int32, (own_blocks, 1), 0)
    select = (tile_ids[None, :] == mine).astype(jnp.float32)
    stacked = tiles.reshape(3, -1, block_width)
    own_share = jnp.einsum("kj,cjb->ckb", select, stacked, precision=lax.Precision.HIGHEST).reshape(
        3, row_count
    )
    response = partner_2(own_share, "grp", 0)
    return (site_result, response)


def solution(mesh):
    in_specs = (
        P(None, ("grp", "dom", "sub")),
        P(("grp", "dom", "sub")),
        P(("grp", "dom", "sub")),
        P(("grp", "dom", "sub"), None),
        P(("grp", "dom", "sub"), None),
        P(None, ("grp", "dom", "sub")),
        P(("grp", "dom", "sub")),
        P(),
        P(),
        P(),
        P(),
        P(),
        P(),
        P(),
    )
    out_specs = (P(None, ("grp", "dom", "sub")), P(None, ("grp", "dom", "sub")))
    return jax.shard_map(local, mesh=mesh, in_specs=in_specs, out_specs=out_specs, check_vma=False)
```

profile of v0, /device:TPU:1, one launch (start us, length us, event | category | flops | bytes accessed | tf_op | source)
XLA Modules:
  0.0 365.2 jit_solution(16709847049985840067)
XLA Ops:
  4.9 5.2 %collective-permute-start.1 = (f32[5,128]{0,1:T(8,128)S(1)}, f32[5,128]{0,1:T(8,128)S(1)}, u32[]{:S(2)}, u32[]{:S(2)}) collective-permute-start(f32[5,128]{0,1:T(8,128)S(1)} %bitcast.279), channel_id=1, source_target_pairs={{0,1},{1,2},{2,3},{3,4},{4,5},{5,6},{6,7},{7,8},{8,9},{9,10},{10,1... | collective-permute-start | bytes 7688 | tf_op jit(solution)/shard_map/ppermute | solution.py:22
  16.6 11.7 %all-reduce = s32[64]{0:T(128)} all-reduce(s32[64]{0:T(128)S(1)} %dynamic-update-slice), channel_id=1, replica_groups=mesh['grp'=2,'dom'=8,'sub'=2] {'dom','sub'}, use_global_device_ids=true, to_apply=%add | all-reduce | flops 64 | bytes 512
  29.3 32.9 %gather_fusion.14 = f32[8192]{0:T(1024)S(1)} fusion(f32[513]{0:T(1024)S(1)} %slice_reduce_fusion, s32[8192]{0:T(1024)S(1)} %broadcast_clamp_fusion.4), kind=kCustom, calls=%fused_computation.14 | custom fusion | bytes 98304 | tf_op jit(solution)/shard_map/gather | solution.py:190
  62.3 27.7 %gather_fusion.9 = f32[8192,3]{1,0:T(8,128)} fusion(f32[3,513]{0,1:T(8,128)S(1)} %copy.124, s32[8192]{0:T(1024)S(1)} %broadcast_clamp_fusion.4), kind=kCustom, calls=%fused_computation.9 | custom fusion | bytes 229376 | tf_op jit(solution)/shard_map/gather | solution.py:148
  90.0 4.5 %multiply_reduce_fusion.4 = (f32[32,256]{1,0:T(8,128)S(1)}, f32[32,256]{1,0:T(8,128)S(1)}, f32[3,32,256]{0,2,1:T(8,128)S(1)}) fusion(f32[3,32,256]{0,2,1:T(8,128)} %bitcast.252, f32[3,256]{0,1:T(8,128)S(1)} %copy.119), kind=kLoop, calls=%fused_computation.156 | loop fusion | flops 106496 | bytes 265216 | tf_op jit(solution)/shard_map/reduce_sum | solution.py:59
  94.5 1.9 copy-done.1
  96.4 2.5 subtract_reduce_fusion.4
  98.9 30.9 %all_gather.9 = f32[5,4096]{1,0:T(8,128)S(1)} all-gather(f32[5,256]{1,0:T(8,128)S(1)} %collective-permute-done), channel_id=1, replica_groups=mesh['grp'=2,'dom'=8,'sub'=2] {'dom','sub'}, dimensions={1}, use_global_device_ids=true | all-gather | bytes 87040 | tf_op jit(solution)/shard_map/all_gather | solution.py:145
  134.7 4.0 %collective-permute-start.7 = (f32[3,128]{0,1:T(8,128)S(1)}, f32[3,128]{0,1:T(8,128)S(1)}, u32[]{:S(2)}, u32[]{:S(2)}) collective-permute-start(f32[3,128]{0,1:T(8,128)S(1)} %bitcast.284), channel_id=1, source_target_pairs={{0,1},{1,2},{2,3},{3,4},{4,5},{5,6},{6,7},{7,8},{8,9},{9,10},{10,1... | collective-permute-start | bytes 4616 | tf_op jit(solution)/shard_map/ppermute | solution.py:22
  140.1 36.5 %conditional.12 = (f32[3,256]{0,1:T(8,128)S(1)}) conditional(s32[]{:T(128)} %convert_element_type.77, (f32[256]{0:T(256)S(1)}, f32[32,256]{1,0:T(8,128)S(1)}, s32[32,256]{1,0:T(8,128)S(1)}, f32[3,513]{1,0:T(4,128)S(1)}, f32[3,32,256]{0,2,1:T(8,128)}, /*index=5*/f32[3,256]{0,1:T(8,128)S(1)}) %tuple.223, f32[3,256]{0,1:T(8,128)S(1)} %get-tuple-element.543), branch_computations={%region_23.26_spmd, %region_26.27_spmd} | conditional | flops 238336 | bytes 1860696 | solution.py:197
  140.3 27.7 %gather_fusion = f32[8192,3]{1,0:T(8,128)} fusion(f32[3,513]{0,1:T(8,128)S(1)} %copy.129, s32[8192]{0:T(1024)S(1)} %broadcast_clamp_fusion), kind=kCustom, calls=%fused_computation.2 | custom fusion | bytes 229376 | tf_op jit(solution)/shard_map/cond/branch_0_fun/gather | solution.py:202
  168.0 4.8 %multiply_reduce_fusion = f32[32,256]{1,0:T(8,128)S(1)} fusion(f32[3,32,256]{0,2,1:T(8,128)} %get-tuple-element.284, f32[3,32,256]{0,2,1:T(8,128)} %bitcast.244), kind=kLoop, calls=%fused_computation.116 | loop fusion | flops 40960 | bytes 229376 | tf_op jit(solution)/shard_map/cond/branch_0_fun/reduce_sum | solution.py:59
  173.9 2.5 subtract_reduce_fusion
  179.2 4.3 %collective-permute-start.9 = (f32[3,128]{0,1:T(8,128)S(1)}, f32[3,128]{0,1:T(8,128)S(1)}, u32[]{:S(2)}, u32[]{:S(2)}) collective-permute-start(f32[3,128]{0,1:T(8,128)S(1)} %bitcast.282), channel_id=1, source_target_pairs={{0,1},{1,2},{2,3},{3,4},{4,5},{5,6},{6,7},{7,8},{8,9},{9,10},{10,1... | collective-permute-start | bytes 4616 | tf_op jit(solution)/shard_map/ppermute | solution.py:22
  184.9 36.5 %conditional.13 = (f32[3,256]{0,1:T(8,128)S(1)}) conditional(s32[]{:T(128)} %convert_element_type.77, (f32[256]{0:T(256)S(1)}, f32[32,256]{1,0:T(8,128)S(1)}, s32[32,256]{1,0:T(8,128)S(1)}, f32[3,513]{1,0:T(4,128)S(1)}, f32[3,32,256]{0,2,1:T(8,128)}, /*index=5*/f32[3,256]{0,1:T(8,128)S(1)}) %tuple.224, f32[3,256]{0,1:T(8,128)S(1)} %get-tuple-element.898), branch_computations={%region_27.30_spmd, %region_30.31_spmd} | conditional | flops 238336 | bytes 1860696 | solution.py:197
  185.1 27.7 %gather_fusion.1 = f32[8192,3]{1,0:T(8,128)} fusion(f32[3,513]{0,1:T(8,128)S(1)} %copy.133, s32[8192]{0:T(1024)S(1)} %broadcast_clamp_fusion.1), kind=kCustom, calls=%fused_computation.3 | custom fusion | bytes 229376 | tf_op jit(solution)/shard_map/cond/branch_0_fun/gather | solution.py:202
  212.9 4.8 %multiply_reduce_fusion.1 = f32[32,256]{1,0:T(8,128)S(1)} fusion(f32[3,32,256]{0,2,1:T(8,128)} %get-tuple-element.290, f32[3,32,256]{0,2,1:T(8,128)} %bitcast.246), kind=kLoop, calls=%fused_computation.126 | loop fusion | flops 40960 | bytes 229376 | tf_op jit(solution)/shard_map/cond/branch_0_fun/reduce_sum | solution.py:59
  218.8 2.5 subtract_reduce_fusion.1
  224.0 4.9 %collective-permute-start.11 = (f32[3,128]{0,1:T(8,128)S(1)}, f32[3,128]{0,1:T(8,128)S(1)}, u32[]{:S(2)}, u32[]{:S(2)}) collective-permute-start(f32[3,128]{0,1:T(8,128)S(1)} %bitcast.280), channel_id=1, source_target_pairs={{0,1},{1,2},{2,3},{3,4},{4,5},{5,6},{6,7},{7,8},{8,9},{9,10},{10,1... | collective-permute-start | bytes 4616 | tf_op jit(solution)/shard_map/ppermute | solution.py:22
  232.1 5.2 %collective-permute-start.3 = (bf16[128,256]{1,0:T(8,128)(2,1)S(1)}, bf16[128,256]{1,0:T(8,128)(2,1)S(1)}, u32[]{:S(2)}, u32[]{:S(2)}) collective-permute-start(bf16[128,256]{1,0:T(8,128)(2,1)S(1)} %gather_fusion.10), channel_id=1, source_target_pairs={{0,1},{1,2},{2,3},{3,4},{4,5},{5,6},{6,7},{7,8},{8,9},{9,10},{10,1... | collective-permute-start | bytes 196616 | tf_op jit(solution)/shard_map/ppermute | solution.py:22
  237.6 36.7 %conditional.14 = (f32[3,256]{0,1:T(8,128)S(1)}) conditional(s32[]{:T(128)} %convert_element_type.77, (f32[256]{0:T(256)S(1)}, f32[32,256]{1,0:T(8,128)S(1)}, s32[32,256]{1,0:T(8,128)S(1)}, f32[3,513]{1,0:T(4,128)S(1)}, f32[3,32,256]{0,2,1:T(8,128)}, /*index=5*/f32[3,256]{0,1:T(8,128)S(1)}) %tuple.225, f32[3,256]{0,1:T(8,128)S(1)} %get-tuple-element.899), branch_computations={%region_31.34_spmd, %region_34.35_spmd} | conditional | flops 238336 | bytes 1860696 | solution.py:197
  238.0 27.7 %gather_fusion.2 = f32[8192,3]{1,0:T(8,128)} fusion(f32[3,513]{0,1:T(8,128)S(1)} %copy.137, s32[8192]{0:T(1024)S(1)} %broadcast_clamp_fusion.2), kind=kCustom, calls=%fused_computation.4 | custom fusion | bytes 229376 | tf_op jit(solution)/shard_map/cond/branch_0_fun/gather | solution.py:202
  265.7 4.8 %multiply_reduce_fusion.2 = f32[32,256]{1,0:T(8,128)S(1)} fusion(f32[3,32,256]{0,2,1:T(8,128)} %get-tuple-element.296, f32[3,32,256]{0,2,1:T(8,128)} %bitcast.248), kind=kLoop, calls=%fused_computation.136 | loop fusion | flops 40960 | bytes 229376 | tf_op jit(solution)/shard_map/cond/branch_0_fun/reduce_sum | solution.py:59
  271.6 2.5 subtract_reduce_fusion.2
  276.9 4.9 %collective-permute-start.13 = (f32[3,128]{0,1:T(8,128)S(1)}, f32[3,128]{0,1:T(8,128)S(1)}, u32[]{:S(2)}, u32[]{:S(2)}) collective-permute-start(f32[3,128]{0,1:T(8,128)S(1)} %bitcast.283), channel_id=1, source_target_pairs={{0,1},{1,2},{2,3},{3,4},{4,5},{5,6},{6,7},{7,8},{8,9},{9,10},{10,1... | collective-permute-start | bytes 4616 | tf_op jit(solution)/shard_map/ppermute | solution.py:22
  286.4 4.9 %collective-permute-start.5 = (bf16[128,256]{1,0:T(8,128)(2,1)S(1)}, bf16[128,256]{1,0:T(8,128)(2,1)S(1)}, u32[]{:S(2)}, u32[]{:S(2)}) collective-permute-start(bf16[128,256]{1,0:T(8,128)(2,1)S(1)} %gather_fusion.12), channel_id=1, source_target_pairs={{0,1},{1,2},{2,3},{3,4},{4,5},{5,6},{6,7},{7,8},{8,9},{9,10},{10,1... | collective-permute-start | bytes 196616 | tf_op jit(solution)/shard_map/ppermute | solution.py:22
  291.3 36.5 %conditional.15 = (f32[3,256]{0,1:T(8,128)S(1)}) conditional(s32[]{:T(128)} %convert_element_type.77, (f32[256]{0:T(256)S(1)}, f32[32,256]{1,0:T(8,128)S(1)}, s32[32,256]{1,0:T(8,128)S(1)}, f32[3,513]{1,0:T(4,128)S(1)}, f32[3,32,256]{0,2,1:T(8,128)}, /*index=5*/f32[3,256]{0,1:T(8,128)S(1)}) %tuple.226, f32[3,256]{0,1:T(8,128)S(1)} %get-tuple-element.900), branch_computations={%region_35.38_spmd, %region_38.39_spmd} | conditional | flops 238336 | bytes 1860696 | solution.py:197
  291.5 27.7 %gather_fusion.3 = f32[8192,3]{1,0:T(8,128)} fusion(f32[3,513]{0,1:T(8,128)S(1)} %copy.141, s32[8192]{0:T(1024)S(1)} %broadcast_clamp_fusion.3), kind=kCustom, calls=%fused_computation.5 | custom fusion | bytes 229376 | tf_op jit(solution)/shard_map/cond/branch_0_fun/gather | solution.py:202
  319.2 4.8 %multiply_reduce_fusion.3 = f32[32,256]{1,0:T(8,128)S(1)} fusion(f32[3,32,256]{0,2,1:T(8,128)} %get-tuple-element.302, f32[3,32,256]{0,2,1:T(8,128)} %bitcast.250), kind=kLoop, calls=%fused_computation.146 | loop fusion | flops 40960 | bytes 229376 | tf_op jit(solution)/shard_map/cond/branch_0_fun/reduce_sum | solution.py:59
  325.2 2.5 subtract_reduce_fusion.3
  328.6 1.8 while.41
  330.5 32.7 %all_gather.10 = f32[3,8192]{1,0:T(4,128)S(1)} all-gather(f32[3,512]{1,0:T(4,128)S(1)} %bitcast.273), channel_id=1, replica_groups=mesh['grp'=2,'dom'=8,'sub'=2] {'dom','sub'}, dimensions={1}, use_global_device_ids=true | all-gather | bytes 104448 | tf_op jit(solution)/shard_map/all_gather | solution.py:212
  (210 shorter events, 45.5 us)
Async XLA Ops:
  0.6 327.4 %copy-start = (bf16[256,2]{0,1:T(2,128)(2,1)S(1)}, bf16[256,2]{0,1:T(2,128)(2,1)}, u32[]{:S(2)}) copy-start(bf16[256,2]{0,1:T(2,128)(2,1)} %param.51) | copy-start | bytes 3076
  1.4 97.6 %collective-permute-start = (f32[5,256]{1,0:T(8,128)S(1)}, f32[5,256]{1,0:T(8,128)S(1)}, u32[]{:S(2)}, u32[]{:S(2)}) collective-permute-start(f32[5,256]{1,0:T(8,128)S(1)} %pad_maximum_fusion), channel_id=1, source_target_pairs={{0,16},{16,0},{1,17},{17,1},{2,18},{18,2},{3,19},{19,3},{4,20},{20... | collective-permute-start | bytes 15368 | tf_op jit(solution)/shard_map/ppermute | solution.py:33
  3.0 25.4 %collective-permute-start.2 = (f32[5,128]{0,1:T(8,128)S(1)}, f32[5,128]{0,1:T(8,128)S(1)}, u32[]{:S(2)}, u32[]{:S(2)}) collective-permute-start(f32[5,128]{0,1:T(8,128)S(1)} %bitcast.278), channel_id=1, source_target_pairs={{1,0},{2,1},{3,2},{4,3},{5,4},{6,5},{7,6},{8,7},{9,8},{10,9},{11,1... | collective-permute-start | bytes 7688 | tf_op jit(solution)/shard_map/ppermute | solution.py:25
  4.9 23.5 %collective-permute-start.1 = (f32[5,128]{0,1:T(8,128)S(1)}, f32[5,128]{0,1:T(8,128)S(1)}, u32[]{:S(2)}, u32[]{:S(2)}) collective-permute-start(f32[5,128]{0,1:T(8,128)S(1)} %bitcast.279), channel_id=1, source_target_pairs={{0,1},{1,2},{2,3},{3,4},{4,5},{5,6},{6,7},{7,8},{8,9},{9,10},{10,1... | collective-permute-start | bytes 7688 | tf_op jit(solution)/shard_map/ppermute | solution.py:22
  94.5 36.0 %copy-start.11 = (f32[3,256]{1,0:T(4,128)S(1)}, f32[3,256]{1,0:T(4,128)}, u32[]{:S(2)}) copy-start(f32[3,256]{1,0:T(4,128)} %param.38) | copy-start | bytes 9220
  130.6 9.5 %copy-start.10 = (s32[256,32]{0,1:T(8,128)S(1)}, s32[256,32]{0,1:T(8,128)}, u32[]{:S(2)}) copy-start(s32[256,32]{0,1:T(8,128)} %param.42) | copy-start | bytes 98308
  133.4 5.4 %collective-permute-start.8 = (f32[3,128]{0,1:T(8,128)S(1)}, f32[3,128]{0,1:T(8,128)S(1)}, u32[]{:S(2)}, u32[]{:S(2)}) collective-permute-start(f32[3,128]{0,1:T(8,128)S(1)} %bitcast.287), channel_id=1, source_target_pairs={{1,0},{2,1},{3,2},{4,3},{5,4},{6,5},{7,6},{8,7},{9,8},{10,9},{11,1... | collective-permute-start | bytes 4616 | tf_op jit(solution)/shard_map/ppermute | solution.py:25
  134.7 5.3 %collective-permute-start.7 = (f32[3,128]{0,1:T(8,128)S(1)}, f32[3,128]{0,1:T(8,128)S(1)}, u32[]{:S(2)}, u32[]{:S(2)}) collective-permute-start(f32[3,128]{0,1:T(8,128)S(1)} %bitcast.284), channel_id=1, source_target_pairs={{0,1},{1,2},{2,3},{3,4},{4,5},{5,6},{6,7},{7,8},{8,9},{9,10},{10,1... | collective-permute-start | bytes 4616 | tf_op jit(solution)/shard_map/ppermute | solution.py:22
  168.0 4.8 %copy-start.2 = (f32[3,32,256]{0,2,1:T(8,128)S(1)}, f32[3,32,256]{0,2,1:T(8,128)}, u32[]{:S(2)}) copy-start(f32[3,32,256]{0,2,1:T(8,128)} %get-tuple-element.284) | copy-start | bytes 294916 | tf_op jit(solution)/shard_map/cond
  168.0 5.9 %copy-start.6 = (f32[8192,3]{1,0:T(8,128)S(1)}, f32[8192,3]{1,0:T(8,128)}, u32[]{:S(2)}) copy-start(f32[8192,3]{1,0:T(8,128)} %gather_fusion) | copy-start | bytes 294916 | tf_op jit(solution)/shard_map/cond
  177.9 5.7 %collective-permute-start.10 = (f32[3,128]{0,1:T(8,128)S(1)}, f32[3,128]{0,1:T(8,128)S(1)}, u32[]{:S(2)}, u32[]{:S(2)}) collective-permute-start(f32[3,128]{0,1:T(8,128)S(1)} %bitcast.285), channel_id=1, source_target_pairs={{1,0},{2,1},{3,2},{4,3},{5,4},{6,5},{7,6},{8,7},{9,8},{10,9},{11,1... | collective-permute-start | bytes 4616 | tf_op jit(solution)/shard_map/ppermute | solution.py:25
  179.2 5.6 %collective-permute-start.9 = (f32[3,128]{0,1:T(8,128)S(1)}, f32[3,128]{0,1:T(8,128)S(1)}, u32[]{:S(2)}, u32[]{:S(2)}) collective-permute-start(f32[3,128]{0,1:T(8,128)S(1)} %bitcast.282), channel_id=1, source_target_pairs={{0,1},{1,2},{2,3},{3,4},{4,5},{5,6},{6,7},{7,8},{8,9},{9,10},{10,1... | collective-permute-start | bytes 4616 | tf_op jit(solution)/shard_map/ppermute | solution.py:22
  184.9 44.0 %copy-start.13 = (bf16[256,256]{1,0:T(8,128)(2,1)S(1)}, bf16[256,256]{1,0:T(8,128)(2,1)}, u32[]{:S(2)}) copy-start(bf16[256,256]{1,0:T(8,128)(2,1)} %param.41) | copy-start | bytes 393220
  184.9 44.0 %copy-start.19 = (f32[256]{0:T(256)S(1)}, f32[256]{0:T(256)}, u32[]{:S(2)}) copy-start(f32[256]{0:T(256)} %param.50) | copy-start | bytes 3076
  184.9 44.1 %copy-start.12 = (bf16[2,256,256]{2,1,0:T(8,128)(2,1)S(1)}, bf16[2,256,256]{2,1,0:T(8,128)(2,1)}, u32[]{:S(2)}) copy-start(bf16[2,256,256]{2,1,0:T(8,128)(2,1)} %param.48) | copy-start | bytes 786436
  212.9 5.9 %copy-start.7 = (f32[8192,3]{1,0:T(8,128)S(1)}, f32[8192,3]{1,0:T(8,128)}, u32[]{:S(2)}) copy-start(f32[8192,3]{1,0:T(8,128)} %gather_fusion.1) | copy-start | bytes 294916 | tf_op jit(solution)/shard_map/cond
  222.7 14.7 %collective-permute-start.12 = (f32[3,128]{0,1:T(8,128)S(1)}, f32[3,128]{0,1:T(8,128)S(1)}, u32[]{:S(2)}, u32[]{:S(2)}) collective-permute-start(f32[3,128]{0,1:T(8,128)S(1)} %bitcast.281), channel_id=1, source_target_pairs={{1,0},{2,1},{3,2},{4,3},{5,4},{6,5},{7,6},{8,7},{9,8},{10,9},{11,1... | collective-permute-start | bytes 4616 | tf_op jit(solution)/shard_map/ppermute | solution.py:25
  224.0 13.5 %collective-permute-start.11 = (f32[3,128]{0,1:T(8,128)S(1)}, f32[3,128]{0,1:T(8,128)S(1)}, u32[]{:S(2)}, u32[]{:S(2)}) collective-permute-start(f32[3,128]{0,1:T(8,128)S(1)} %bitcast.280), channel_id=1, source_target_pairs={{0,1},{1,2},{2,3},{3,4},{4,5},{5,6},{6,7},{7,8},{8,9},{9,10},{10,1... | collective-permute-start | bytes 4616 | tf_op jit(solution)/shard_map/ppermute | solution.py:22
  230.8 52.3 %collective-permute-start.4 = (bf16[128,256]{1,0:T(8,128)(2,1)S(1)}, bf16[128,256]{1,0:T(8,128)(2,1)S(1)}, u32[]{:S(2)}, u32[]{:S(2)}) collective-permute-start(bf16[128,256]{1,0:T(8,128)(2,1)S(1)} %gather_fusion.11), channel_id=1, source_target_pairs={{1,0},{2,1},{3,2},{4,3},{5,4},{6,5},{7,6},{8,7},{9,8},{10,9},{11,1... | collective-permute-start | bytes 196616 | tf_op jit(solution)/shard_map/ppermute | solution.py:25
  232.1 51.1 %collective-permute-start.3 = (bf16[128,256]{1,0:T(8,128)(2,1)S(1)}, bf16[128,256]{1,0:T(8,128)(2,1)S(1)}, u32[]{:S(2)}, u32[]{:S(2)}) collective-permute-start(bf16[128,256]{1,0:T(8,128)(2,1)S(1)} %gather_fusion.10), channel_id=1, source_target_pairs={{0,1},{1,2},{2,3},{3,4},{4,5},{5,6},{6,7},{7,8},{8,9},{9,10},{10,1... | collective-permute-start | bytes 196616 | tf_op jit(solution)/shard_map/ppermute | solution.py:22
  237.6 45.7 %copy-start.14 = (bf16[2,2,64,64]{3,2,1,0:T(8,128)(2,1)S(1)}, bf16[2,2,64,64]{3,2,1,0:T(8,128)(2,1)}, u32[]{:S(2)}) copy-start(bf16[2,2,64,64]{3,2,1,0:T(8,128)(2,1)} %param.46) | copy-start | bytes 98308
  237.6 45.7 %copy-start.15 = (bf16[2,64,256]{2,1,0:T(8,128)(2,1)S(1)}, bf16[2,64,256]{2,1,0:T(8,128)(2,1)}, u32[]{:S(2)}) copy-start(bf16[2,64,256]{2,1,0:T(8,128)(2,1)} %param.47) | copy-start | bytes 196612
  237.6 45.7 %copy-start.18 = (bf16[2,8,64]{2,1,0:T(8,128)(2,1)S(1)}, bf16[2,8,64]{2,1,0:T(8,128)(2,1)}, u32[]{:S(2)}) copy-start(bf16[2,8,64]{2,1,0:T(8,128)(2,1)} %param.45) | copy-start | bytes 6148
  265.7 5.9 %copy-start.8 = (f32[8192,3]{1,0:T(8,128)S(1)}, f32[8192,3]{1,0:T(8,128)}, u32[]{:S(2)}) copy-start(f32[8192,3]{1,0:T(8,128)} %gather_fusion.2) | copy-start | bytes 294916 | tf_op jit(solution)/shard_map/cond
  275.6 6.4 %collective-permute-start.14 = (f32[3,128]{0,1:T(8,128)S(1)}, f32[3,128]{0,1:T(8,128)S(1)}, u32[]{:S(2)}, u32[]{:S(2)}) collective-permute-start(f32[3,128]{0,1:T(8,128)S(1)} %bitcast.286), channel_id=1, source_target_pairs={{1,0},{2,1},{3,2},{4,3},{5,4},{6,5},{7,6},{8,7},{9,8},{10,9},{11,1... | collective-permute-start | bytes 4616 | tf_op jit(solution)/shard_map/ppermute | solution.py:25
  276.9 6.2 %collective-permute-start.13 = (f32[3,128]{0,1:T(8,128)S(1)}, f32[3,128]{0,1:T(8,128)S(1)}, u32[]{:S(2)}, u32[]{:S(2)}) collective-permute-start(f32[3,128]{0,1:T(8,128)S(1)} %bitcast.283), channel_id=1, source_target_pairs={{0,1},{1,2},{2,3},{3,4},{4,5},{5,6},{6,7},{7,8},{8,9},{9,10},{10,1... | collective-permute-start | bytes 4616 | tf_op jit(solution)/shard_map/ppermute | solution.py:22
  285.1 42.7 %collective-permute-start.6 = (bf16[128,256]{1,0:T(8,128)(2,1)S(1)}, bf16[128,256]{1,0:T(8,128)(2,1)S(1)}, u32[]{:S(2)}, u32[]{:S(2)}) collective-permute-start(bf16[128,256]{1,0:T(8,128)(2,1)S(1)} %gather_fusion.13), channel_id=1, source_target_pairs={{1,0},{2,1},{3,2},{4,3},{5,4},{6,5},{7,6},{8,7},{9,8},{10,9},{11,1... | collective-permute-start | bytes 196616 | tf_op jit(solution)/shard_map/ppermute | solution.py:25
  286.4 41.4 %collective-permute-start.5 = (bf16[128,256]{1,0:T(8,128)(2,1)S(1)}, bf16[128,256]{1,0:T(8,128)(2,1)S(1)}, u32[]{:S(2)}, u32[]{:S(2)}) collective-permute-start(bf16[128,256]{1,0:T(8,128)(2,1)S(1)} %gather_fusion.12), channel_id=1, source_target_pairs={{0,1},{1,2},{2,3},{3,4},{4,5},{5,6},{6,7},{7,8},{8,9},{9,10},{10,1... | collective-permute-start | bytes 196616 | tf_op jit(solution)/shard_map/ppermute | solution.py:22
  319.2 5.9 %copy-start.9 = (f32[8192,3]{1,0:T(8,128)S(1)}, f32[8192,3]{1,0:T(8,128)}, u32[]{:S(2)}) copy-start(f32[8192,3]{1,0:T(8,128)} %gather_fusion.3) | copy-start | bytes 294916 | tf_op jit(solution)/shard_map/cond
  328.0 35.3 %copy-start.20 = (s32[2]{0:T(128)S(1)}, s32[2]{0:T(128)}, u32[]{:S(2)}) copy-start(s32[2]{0:T(128)} %iota_add_fusion) | copy-start | bytes 28
  328.0 35.3 %copy-start.21 = (s32[64]{0:T(128)S(1)}, s32[64]{0:T(128)}, u32[]{:S(2)}) copy-start(s32[64]{0:T(128)} %all-reduce) | copy-start | bytes 772
  363.4 1.2 collective-permute-start.15
  (6 other events, 18.4 us)
where the time goes:
time: 366 us; the launch traced here: 365 us
  local copies, waits for them, and re-layouts  195 us (53%)
  blocking collectives  75.4 us (21%)
  other arithmetic  45 us (12%)
  starting transfers between devices  42.5 us (12%)
  waiting for transfers between devices  3.85 us (1%)
    gather x4, local copies, waits for them, and re-layouts, local(): t[:, slot_major]  111 us
    ppermute x7, starting transfers between devices, with_halo(): lax.ppermute(lax.slice_in_dim(block, block.shape[dim] - width, None, axis...  33.4 us
    gather x2, local copies, waits for them, and re-layouts, local(): site_table[3][slot_major]  32.9 us
    all_gather x1, blocking collectives, local(): lax.all_gather(response_term, ('dom', 'sub'), axis=1, tiled=True)  32.7 us
    all_gather x1, blocking collectives, local(): others = lax.all_gather(partner, ('dom', 'sub'), axis=1, tiled=True)  30.9 us
    gather x1, local copies, waits for them, and re-layouts, local(): offset = positions[:, None, :] - site_table[:3][:, slot_major]  27.7 us
    reduce_sum x5, other arithmetic, slot_field(): projected = jnp.sum(offset * source_dipole, axis=0)  23.5 us
    reduce_sum x5, other arithmetic, slot_field(): jnp.sum(offset * source_scale[None] - source_dipole * inverse_cube[None],...  12.5 us
  transfers between devices with their start and end apart: 16, of which 4 were waited for; matrix products, arithmetic and copies ran while one was open for 42% of the time, Pallas kernels for 0%

commit v1 on v0

v1 whole, which is shorter than its diff:
```python
import functools

import jax
import jax.numpy as jnp
from jax import lax
from jax.experimental import pallas as pl
from jax.experimental.pallas import tpu as pltpu
from jax.sharding import PartitionSpec as P

SWEEPS = 4
BLOCK = 128
SMOOTH = 1.0
SPACING = 0.75
MESH = pl.DeviceIdType.MESH
F32 = jnp.float32
BF16 = jnp.bfloat16


def silu(x):
    return x * (0.5 + 0.5 * jnp.tanh(0.5 * x))


def lane_pick(rows, index):
    shape = index.shape
    return jnp.take_along_axis(
        jnp.broadcast_to(rows, shape), index, axis=1, mode="promise_in_bounds"
    )


def table_gather(pieces, local, chunk):
    total = jnp.zeros(local.shape, F32)
    for number, rows in pieces:
        total = jnp.where(chunk == number, lane_pick(rows, local), total)
    return total


def kernel(
    n_dom,
    n_sub,
    positions,
    charges,
    polar,
    features,
    neighbours,
    send_rows,
    blocks,
    radial_in,
    radial_mid,
    radial_out,
    node_in,
    node_out,
    field_gain,
    readout,
    site_result,
    response,
    packet,
    everyone,
    near_rows,
    near_cols,
    own_rows,
    own_cols,
    extra_cols,
    rim_out,
    rim_in,
    index_rows,
    geometry,
    hot,
    third,
    wide_in,
    wide_mid,
    wide_out,
    tables,
    lent,
    hidden_ref,
    acc,
    outside,
    term_out,
    term_in,
    all_send,
    all_recv,
    rim_send,
    rim_recv,
    lift_send,
    lift_recv,
    term_send,
    term_recv,
):
    g = lax.axis_index("grp")
    p = lax.axis_index("dom") * n_sub + lax.axis_index("sub")
    n = n_dom * n_sub
    rows = positions.shape[1]
    own_blocks = rows // BLOCK
    slots = neighbours.shape[1]
    listed = blocks.shape[0]
    layers, basis, radial = radial_in.shape
    channels = features.shape[1]
    rim = send_rows.shape[1]
    pack = channels // radial
    groups = slots // pack
    other = 1 - g

    def place(group, q):
        return (group, lax.div(q, n_sub), lax.rem(q, n_sub))

    def peer(i):
        return lax.rem(p + i, n)

    barrier = pltpu.get_barrier_semaphore()

    @pl.loop(0, n)
    def _(i):
        pl.semaphore_signal(barrier, inc=1, device_id=place(other, peer(i)), device_id_type=MESH)

    @pl.when(p > 0)
    def _():
        pl.semaphore_signal(barrier, inc=1, device_id=place(g, p - 1), device_id_type=MESH)

    @pl.when(p < n - 1)
    def _():
        pl.semaphore_signal(barrier, inc=1, device_id=place(g, p + 1), device_id_type=MESH)

    own_rows[...] = jnp.zeros_like(own_rows)
    own_rows[0:3, :] = positions[...]
    own_rows[3:4, :] = charges[...]
    own = own_rows[...]
    for b in range(own_blocks):
        packet[b] = own[:, b * BLOCK : (b + 1) * BLOCK]

    def fill_rims(step, values):
        for side in range(2):
            index = jnp.broadcast_to(send_rows[side : side + 1, :], (8, rim))
            rim_out[step, side] = table_gather(
                [(c, values[:, c * BLOCK : (c + 1) * BLOCK]) for c in range(own_blocks)],
                index & (BLOCK - 1),
                lax.shift_right_logical(index, 7),
            )

    def side_copy(src, dst, send, recv, step, side, q):
        return pltpu.make_async_remote_copy(
            src_ref=src,
            dst_ref=dst,
            send_sem=send.at[step, side],
            recv_sem=recv.at[step, side],
            device_id=place(g, q),
            device_id_type=MESH,
        )

    def rim_copy(step, side, q):
        return side_copy(
            rim_out.at[step, side], rim_in.at[step, side], rim_send, rim_recv, step, side, q
        )

    def lift_copy(layer, side, q):
        return side_copy(
            lent.at[layer, side],
            tables.at[layer, pl.ds(rows + side * rim, rim)],
            lift_send,
            lift_recv,
            layer,
            side,
            q,
        )

    def start(copy, step):
        @pl.when(p < n - 1)
        def _():
            copy(step, 0, p + 1).start()

        @pl.when(p > 0)
        def _():
            copy(step, 1, p - 1).start()

    def arrive(copy, step):
        @pl.when(p > 0)
        def _():
            copy(step, 0, p - 1).wait_recv()

        @pl.when(p < n - 1)
        def _():
            copy(step, 1, p + 1).wait_recv()

    def gone(copy, step):
        @pl.when(p < n - 1)
        def _():
            copy(step, 0, p + 1).wait_send()

        @pl.when(p > 0)
        def _():
            copy(step, 1, p - 1).wait_send()

    fill_rims(0, own)

    @pl.when(p == 0)
    def _():
        for step in range(1 + SWEEPS):
            rim_in[step, 0] = jnp.zeros((8, rim), F32)
        for layer in range(layers):
            tables[layer, rows : rows + rim] = jnp.zeros((rim, channels), BF16)

    @pl.when(p == n - 1)
    def _():
        for step in range(1 + SWEEPS):
            rim_in[step, 1] = jnp.zeros((8, rim), F32)
        for layer in range(layers):
            tables[layer, rows + rim :] = jnp.zeros((rim, channels), BF16)

    pl.semaphore_wait(barrier, n + (p > 0).astype(jnp.int32) + (p < n - 1).astype(jnp.int32))

    def packet_copy(i):
        return pltpu.make_async_remote_copy(
            src_ref=packet,
            dst_ref=everyone.at[pl.ds(p * own_blocks, own_blocks)],
            send_sem=all_send,
            recv_sem=all_recv,
            device_id=place(other, peer(i)),
            device_id_type=MESH,
        )

    start(rim_copy, 0)

    @pl.loop(0, n)
    def _(i):
        packet_copy(i).start()

    wide = jnp.concatenate(
        [neighbours[...].astype(F32), jnp.zeros((rows, BLOCK - slots), F32)], axis=1
    )
    index_rows[...] = wide.T[:slots, :].astype(jnp.int32)
    own_cols[...] = own.T

    @pl.when(g == 0)
    def _():
        lane = lax.broadcasted_iota(jnp.int32, (rows, rows + 2 * rim), 1)
        for k in range(slots):
            hot[k] = jnp.where(neighbours[:, k : k + 1] == lane, 1.0, 0.0).astype(BF16)
        spread_r = (
            lax.broadcasted_iota(jnp.int32, (channels, radial), 0) % radial
            == lax.broadcasted_iota(jnp.int32, (channels, radial), 1)
        ).astype(F32).astype(BF16)
        spread_c = (
            lax.broadcasted_iota(jnp.int32, (radial, channels), 1) % radial
            == lax.broadcasted_iota(jnp.int32, (radial, channels), 0)
        ).astype(F32).astype(BF16)
        same_in = (
            lax.broadcasted_iota(jnp.int32, (pack * basis, channels), 0) // basis
            == lax.broadcasted_iota(jnp.int32, (pack * basis, channels), 1) // radial
        )
        same_mid = (
            lax.broadcasted_iota(jnp.int32, (channels, channels), 0) // radial
            == lax.broadcasted_iota(jnp.int32, (channels, channels), 1) // radial
        )
        for layer in range(layers):
            flat = jnp.dot(radial_in[layer], spread_c, preferred_element_type=F32)
            wide_in[layer] = jnp.where(
                same_in, jnp.concatenate([flat] * pack, axis=0), 0.0
            ).astype(BF16)
            for m in range(2):
                flat = jnp.dot(
                    jnp.dot(spread_r, radial_mid[layer, m], preferred_element_type=F32).astype(
                        BF16
                    ),
                    spread_c,
                    preferred_element_type=F32,
                )
                wide_mid[layer, m] = jnp.where(same_mid, flat, 0.0).astype(BF16)
            for j in range(pack):
                wide_out[layer, j] = jnp.zeros((channels, channels), BF16)
                wide_out[layer, j, j * radial : (j + 1) * radial, :] = radial_out[layer]

    pltpu.make_async_copy(everyone, everyone, all_recv).wait()
    for l in range(listed):
        tile = everyone[blocks[l]]
        near_rows[:, l * BLOCK : (l + 1) * BLOCK] = tile
        near_cols[l * BLOCK : (l + 1) * BLOCK, :] = tile.T

    def field(targets, source_cols, count, charge, dipole):
        x, y, z = (targets[c : c + 1, :] for c in range(3))
        width = targets.shape[1]

        def step(i, sums):
            at = pl.ds(pl.multiple_of(i * 8, 8), 8)
            source = source_cols[at, :]
            rx = x - source[:, 0:1]
            ry = y - source[:, 1:2]
            rz = z - source[:, 2:3]
            w = lax.rsqrt(rx * rx + ry * ry + rz * rz + SMOOTH)
            w2 = w * w
            w3 = w2 * w
            if not dipole:
                s = charge(at, source) * w3
                return (sums[0] + rx * s, sums[1] + ry * s, sums[2] + rz * s)
            d = extra_cols[at, :]
            dx, dy, dz = d[:, 0:1], d[:, 1:2], d[:, 2:3]
            s = 3.0 * (rx * dx + ry * dy + rz * dz) * (w3 * w2)
            return (
                sums[0] + (rx * s - dx * w3),
                sums[1] + (ry * s - dy * w3),
                sums[2] + (rz * s - dz * w3),
            )

        zero = jnp.zeros((8, width), F32)
        sums = lax.fori_loop(0, count // 8, step, (zero, zero, zero), unroll=4)
        return [jnp.sum(s, axis=0, keepdims=True) for s in sums]

    out = field(own, near_cols, listed * BLOCK, lambda at, source: source[:, 3:4], False)
    for c in range(3):
        outside[c : c + 1, :] = out[c]

    def edges():
        arrive(rim_copy, 0)
        for tile in range(own_blocks):
            at = slice(tile * BLOCK, (tile + 1) * BLOCK)
            index = index_rows[:, at]
            local = index & (BLOCK - 1)
            chunk = lax.shift_right_logical(index, 7)
            picked = []
            for c in range(4):
                pieces = [
                    (b, own_rows[c : c + 1, b * BLOCK : (b + 1) * BLOCK])
                    for b in range(own_blocks)
                ] + [(own_blocks + side, rim_in[0, side, c : c + 1, :]) for side in range(2)]
                picked.append(table_gather(pieces, local, chunk))
            ox, oy, oz = (own_rows[c : c + 1, at] - picked[c] for c in range(3))
            dist_sq = ox * ox + oy * oy + oz * oz + SMOOTH
            yield at, (ox, oy, oz), dist_sq, picked[3], local, chunk

    def send_terms(charge, dipole):
        width = listed * BLOCK
        for half in range(0, width, 2 * BLOCK):
            out = field(
                near_rows[:, half : half + 2 * BLOCK], own_cols, rows, charge, dipole
            )
            for c in range(3):
                for l in range(2):
                    term_out[c * listed + half // BLOCK + l] = out[c][
                        0, l * BLOCK : (l + 1) * BLOCK
                    ]

    @pl.when(g == 0)
    def _():
        fx, fy, fz = out
        strength = jnp.sqrt(1.0 + fx * fx + fy * fy + fz * fz)
        site_result[2:3, :] = strength
        strength_col = jnp.broadcast_to(strength, (8, rows)).T[:, 0:1]
        hidden_ref[...] = (features[...].astype(F32) + strength_col * field_gain[...]).astype(BF16)

        def lift(layer):
            lifted = jnp.dot(
                hidden_ref[...], node_in[layer], preferred_element_type=F32
            ).astype(BF16)
            site = lax.broadcasted_iota(jnp.int32, (rows, rim), 0)
            for side in range(2):
                pick = jnp.where(site == send_rows[side : side + 1, :], 1.0, 0.0).astype(BF16)
                lent[layer, side] = lax.dot_general(
                    pick, lifted, (((0,), (0,)), ((), ())), preferred_element_type=F32
                ).astype(BF16)
            start(lift_copy, layer)
            tables[layer, 0:rows] = lifted

        lift(0)
        for at, _, dist_sq, _, _, _ in edges():
            geometry[0, :, at] = jnp.sqrt(dist_sq)

        centre = lax.broadcasted_iota(jnp.int32, (basis, rows), 0).astype(F32) * SPACING

        def radial_step(q, layer):
            parts = []
            for j in range(pack):
                away = jnp.broadcast_to(geometry[0, pl.ds(q * pack + j, 1), :], (basis, rows))
                away = away - centre
                parts.append(jnp.exp(-(away * away)))
            wave = jnp.concatenate(parts, axis=0).astype(BF16)
            h = lax.dot_general(
                wave, wide_in[layer], (((0,), (0,)), ((), ())), preferred_element_type=F32
            )
            h = silu(h).astype(BF16)
            for m in range(2):
                h = silu(jnp.dot(h, wide_mid[layer, m], preferred_element_type=F32)).astype(BF16)
            third[layer, q] = h

        for layer in range(layers):

            @pl.loop(0, groups)
            def _(q):
                radial_step(q, layer)

        for layer in range(layers):
            if layer:
                lift(layer)
            arrive(lift_copy, layer)
            acc[...] = jnp.zeros_like(acc)

            @pl.loop(0, groups)
            def _(q):
                h = third[layer, q]
                table = tables[layer]
                total = None
                for j in range(pack):
                    edge_weight = jnp.dot(h, wide_out[layer, j], preferred_element_type=F32)
                    source = jnp.dot(hot[q * pack + j], table, preferred_element_type=F32)
                    part = edge_weight * source
                    total = part if total is None else total + part
                acc[...] += total

            message = (acc[...] * (1.0 / slots)).astype(BF16)
            update = silu(jnp.dot(message, node_out[layer], preferred_element_type=F32))
            hidden_ref[...] = (hidden_ref[...].astype(F32) + update).astype(BF16)

        readouts = jnp.dot(hidden_ref[...], readout[...], preferred_element_type=F32)
        extra_cols[:, 0:2] = readouts
        padded = jnp.concatenate([readouts, jnp.zeros((rows, BLOCK - 2), F32)], axis=1)
        site_result[0:2, :] = padded.T[0:2, :]
        send_terms(lambda at, source: extra_cols[at, 0:1], False)
        for layer in range(layers):
            gone(lift_copy, layer)

    @pl.when(g == 1)
    def _():
        for at, offset, dist_sq, source_charge, _, _ in edges():
            w = lax.rsqrt(dist_sq)
            w2 = w * w
            w3 = w2 * w
            s = source_charge * w3
            for c in range(3):
                geometry[c, :, at] = offset[c]
                extra = jnp.sum(offset[c] * s, axis=0, keepdims=True)
                outside[c : c + 1, at] = outside[c : c + 1, at] + extra
            geometry[3, :, at] = w3
            geometry[4, :, at] = 3.0 * (w3 * w2)
        gain = polar[...]
        dipole = [gain * outside[c : c + 1, :] for c in range(3)]
        for sweep in range(SWEEPS):
            step = 1 + sweep
            stacked = jnp.concatenate(dipole + [jnp.zeros((5, rows), F32)], axis=0)
            fill_rims(step, stacked)
            start(rim_copy, step)
            arrive(rim_copy, step)
            fresh = [[], [], []]
            for tile in range(own_blocks):
                at = slice(tile * BLOCK, (tile + 1) * BLOCK)
                index = index_rows[:, at]
                local = index & (BLOCK - 1)
                chunk = lax.shift_right_logical(index, 7)
                d = []
                for c in range(3):
                    pieces = [
                        (b, dipole[c][:, b * BLOCK : (b + 1) * BLOCK]) for b in range(own_blocks)
                    ] + [
                        (own_blocks + side, rim_in[step, side, c : c + 1, :]) for side in range(2)
                    ]
                    d.append(table_gather(pieces, local, chunk))
                r = [geometry[c, :, at] for c in range(3)]
                w3 = geometry[3, :, at]
                s = (r[0] * d[0] + r[1] * d[1] + r[2] * d[2]) * geometry[4, :, at]
                for c in range(3):
                    total = jnp.sum(r[c] * s - d[c] * w3, axis=0, keepdims=True)
                    fresh[c].append(gain[:, at] * (outside[c : c + 1, at] + total))
            dipole = [jnp.concatenate(f, axis=1) for f in fresh]
        for c in range(3):
            site_result[c : c + 1, :] = dipole[c]
        stacked = jnp.concatenate(dipole + [jnp.zeros((5, rows), F32)], axis=0)
        extra_cols[...] = stacked.T
        send_terms(None, True)
        for sweep in range(SWEEPS):
            gone(rim_copy, 1 + sweep)

    for l in range(listed):
        term_out[3 * listed + l] = jnp.full((BLOCK,), blocks[l].astype(F32), F32)

    def term_copy(i):
        return pltpu.make_async_remote_copy(
            src_ref=term_out,
            dst_ref=term_in.at[p],
            send_sem=term_send,
            recv_sem=term_recv,
            device_id=place(other, peer(i)),
            device_id_type=MESH,
        )

    @pl.loop(0, n)
    def _(i):
        term_copy(i).start()

    gone(rim_copy, 0)
    pltpu.make_async_copy(everyone, everyone, all_send).wait()
    pltpu.make_async_copy(term_in, term_in, term_recv).wait()

    zero = tuple(jnp.zeros((listed, BLOCK), F32) for _ in range(3 * own_blocks))

    def collect(i, sums):
        terms = term_in[i]
        ids = terms[3 * listed :, :]
        fresh = []
        for b in range(own_blocks):
            mine = (p * own_blocks + b).astype(F32) == ids
            for c in range(3):
                fresh.append(
                    sums[b * 3 + c]
                    + jnp.where(mine, terms[c * listed : (c + 1) * listed, :], 0.0)
                )
        return tuple(fresh)

    sums = lax.fori_loop(0, n, collect, zero)
    for b in range(own_blocks):
        for c in range(3):
            response[c : c + 1, b * BLOCK : (b + 1) * BLOCK] = jnp.sum(
                sums[b * 3 + c], axis=0, keepdims=True
            )
    pltpu.make_async_copy(term_in, term_in, term_send).wait()


def local(n_dom, n_sub, *args):
    (
        positions,
        charges,
        polar,
        features,
        neighbours,
        send_rows,
        blocks,
        radial_in,
        radial_mid,
        radial_out,
        node_in,
        node_out,
        field_gain,
        readout,
    ) = args
    n = n_dom * n_sub
    rows = positions.shape[1]
    own_blocks = rows // BLOCK
    slots = neighbours.shape[1]
    listed = blocks.shape[0]
    layers, basis, radial = radial_in.shape
    channels = features.shape[1]
    rim = send_rows.shape[1]
    pack = channels // radial
    vmem = pl.BlockSpec(memory_space=pltpu.VMEM)
    specs = [vmem] * 14
    specs[6] = pl.BlockSpec(memory_space=pltpu.SMEM)
    dma = pltpu.SemaphoreType.DMA
    return pl.pallas_call(
        functools.partial(kernel, n_dom, n_sub),
        out_shape=(
            jax.ShapeDtypeStruct((3, rows), F32),
            jax.ShapeDtypeStruct((3, rows), F32),
        ),
        in_specs=specs,
        out_specs=(vmem, vmem),
        scratch_shapes=[
            pltpu.VMEM((own_blocks, 8, BLOCK), F32),
            pltpu.VMEM((n * own_blocks, 8, BLOCK), F32),
            pltpu.VMEM((8, listed * BLOCK), F32),
            pltpu.VMEM((listed * BLOCK, 8), F32),
            pltpu.VMEM((8, rows), F32),
            pltpu.VMEM((rows, 8), F32),
            pltpu.VMEM((rows, 8), F32),
            pltpu.VMEM((1 + SWEEPS, 2, 8, rim), F32),
            pltpu.VMEM((1 + SWEEPS, 2, 8, rim), F32),
            pltpu.VMEM((slots, rows), jnp.int32),
            pltpu.VMEM((5, slots, rows), F32),
            pltpu.VMEM((slots, rows, rows + 2 * rim), BF16),
            pltpu.VMEM((layers, slots // pack, rows, channels), BF16),
            pltpu.VMEM((layers, pack * basis, channels), BF16),
            pltpu.VMEM((layers, 2, channels, channels), BF16),
            pltpu.VMEM((layers, pack, channels, channels), BF16),
            pltpu.VMEM((layers, rows + 2 * rim, channels), BF16),
            pltpu.VMEM((layers, 2, rim, channels), BF16),
            pltpu.VMEM((rows, channels), BF16),
            pltpu.VMEM((rows, channels), F32),
            pltpu.VMEM((3, rows), F32),
            pltpu.VMEM((4 * listed, BLOCK), F32),
            pltpu.VMEM((n, 4 * listed, BLOCK), F32),
            dma(()),
            dma(()),
            dma((1 + SWEEPS, 2)),
            dma((1 + SWEEPS, 2)),
            dma((layers, 2)),
            dma((layers, 2)),
            dma(()),
            dma(()),
        ],
        compiler_params=pltpu.CompilerParams(
            collective_id=0, has_side_effects=True, vmem_limit_bytes=56 * 2**20
        ),
    )(
        positions,
        charges.reshape(1, -1),
        polar.reshape(1, -1),
        features,
        neighbours,
        send_rows,
        blocks,
        radial_in,
        radial_mid,
        radial_out,
        node_in,
        node_out,
        field_gain.reshape(1, -1),
        readout,
    )


def solution(mesh):
    sites = ("grp", "dom", "sub")
    in_specs = (
        P(None, sites),
        P(sites),
        P(sites),
        P(sites, None),
        P(sites, None),
        P(None, sites),
        P(sites),
    ) + (P(),) * 7
    out_specs = (P(None, sites), P(None, sites))
    body = functools.partial(local, mesh.shape["dom"], mesh.shape["sub"])
    return jax.shard_map(body, mesh=mesh, in_specs=in_specs, out_specs=out_specs, check_vma=False)
```

time: 366 us -> 50.7 us (0.14)
  local copies, waits for them, and re-layouts: 195 us -> 4.04 us
  blocking collectives: 75.4 us -> 0 us
  Pallas kernels: 0 us -> 45.7 us
  other arithmetic: 45 us -> 0 us
  starting transfers between devices: 42.5 us -> 0 us
  waiting for transfers between devices: 3.85 us -> 0 us
    gather x22 -> x0, local copies, waits for them, and re-layouts: 182 us -> none  [the longest x4 111 us: local(): t[:, slot_major]]
    all_gather x2 -> x0, blocking collectives: 63.7 us -> none  [the longest x1 32.7 us: local(): lax.all_gather(response_term, ('dom', 'sub'), axis=1, tiled=True)]
    pallas_call x0 -> x1, Pallas kernels: none -> 45.7 us  [local(): pl.pallas_call(functools.partial(kernel, n_dom, n_sub), out_shape=(jax.Sh...]
    ppermute x16 -> x0, starting transfers between devices: 42.5 us -> none  [the longest x7 33.4 us: with_halo(): lax.ppermute(lax.slice_in_dim(block, block.shape[dim] - width, None, axis...]
    reduce_sum x23 -> x0, other arithmetic: 38.3 us -> none  [the longest x5 23.5 us: slot_field(): projected = jnp.sum(offset * source_dipole, axis=0)]
    unnamed x1 -> x0, blocking collectives: 11.7 us -> none
    cond x23 -> x0, local copies, waits for them, and re-layouts: 4.79 us -> none
    ppermute x16 -> x0, waiting for transfers between devices: 3.85 us -> none  [the longest x7 3.34 us: with_halo(): lax.ppermute(lax.slice_in_dim(block, block.shape[dim] - width, None, axis...]
  transfers between devices with their start and end apart: 16 -> 0, of which waited for: 4 -> 0; matrix products, arithmetic and copies ran while one was open for 42% -> 0% of each run, Pallas kernels for 0% -> 0%
where the time goes in v1:
time: 50.7 us; the launch traced here: 50.4 us
  Pallas kernels  45.7 us (90%)
  local copies, waits for them, and re-layouts  4.04 us (8%)
  between operations  0.66 us (1%)
    pallas_call x1, Pallas kernels, local(): pl.pallas_call(functools.partial(kernel, n_dom, n_sub), out_shape=(jax.Sh...  45.7 us
    unnamed x10, local copies, waits for them, and re-layouts  4.04 us

profile of v1, /device:TPU:1, one launch (start us, length us, event | category | flops | bytes accessed | tf_op | source)
XLA Modules:
  0.0 50.4 jit_solution(7143882465452147851)
XLA Ops:
  0.6 0.0 copy-start.2
  0.6 0.7 %copy-done.2 = bf16[256,2]{0,1:T(2,128)(2,1)S(1)} copy-done((bf16[256,2]{0,1:T(2,128)(2,1)S(1)}, bf16[256,2]{0,1:T(2,128)(2,1)}, u32[]{:S(2)}) %copy-start.2) | copy-done | bytes 1048
  1.3 0.0 copy-start
  1.3 0.7 %copy.17.readout = bf16[256,2]{1,0:T(8,128)(2,1)} copy(bf16[256,2]{0,1:T(2,128)(2,1)S(1)} %copy-done.2) | data formatting | bytes 2048 | tf_op args[13]
  2.1 0.0 copy-done
  2.1 0.7 %copy.16.neighbours = s32[256,32]{1,0:T(8,128)} copy(s32[256,32]{0,1:T(8,128)S(1)} %copy-done) | data formatting | bytes 65536 | tf_op args[4]
  2.8 45.7 %shard_map.149 = (f32[3,256]{1,0:T(4,128)}, f32[3,256]{1,0:T(4,128)}) custom-call(f32[3,256]{1,0:T(4,128)} %positions.1, f32[1,256]{1,0:T(1,128)} %bitcast.3, f32[1,256]{1,0:T(1,128)} %bitcast.4, bf16[256,256]{1,0:T(8,128)(2,1)} %features.1, s32[256,32]{1,0:T(8,128)} %copy.16.neighbours, s32[2,128]{1,0:T(2,128)} %send_rows.1, s32[4]{0:T(128)} %blocks.1, ...), custom_call_target="tpu_custom_call" | custom-call | tf_op jit(solution)/shard_map/pallas_call | solution.py:542
  48.5 0.0 copy-start.1
  48.6 1.3 %copy.20 = f32[3,256]{1,0:T(4,128)} copy(f32[3,256]{1,0:T(4,128)} %get-tuple-element.4) | data formatting | bytes 6144
  49.8 0.0 copy-done.1
  49.8 0.6 %copy.21 = f32[3,256]{1,0:T(4,128)} copy(f32[3,256]{1,0:T(4,128)S(1)} %copy-done.1) | data formatting | bytes 6144
Async XLA Ops:
  0.6 0.7 %copy-start.2 = (bf16[256,2]{0,1:T(2,128)(2,1)S(1)}, bf16[256,2]{0,1:T(2,128)(2,1)}, u32[]{:S(2)}) copy-start(bf16[256,2]{0,1:T(2,128)(2,1)} %param.27) | copy-start | bytes 3076
  1.3 0.8 %copy-start = (s32[256,32]{0,1:T(8,128)S(1)}, s32[256,32]{0,1:T(8,128)}, u32[]{:S(2)}) copy-start(s32[256,32]{0,1:T(8,128)} %param.18) | copy-start | bytes 98308
  48.5 1.3 %copy-start.1 = (f32[3,256]{1,0:T(4,128)S(1)}, f32[3,256]{1,0:T(4,128)}, u32[]{:S(2)}) copy-start(f32[3,256]{1,0:T(4,128)} %get-tuple-element.5) | copy-start | bytes 9220

commit v2 on v1

--- a/solution.py
+++ b/solution.py
@@ -51,8 +51,7 @@
     node_out,
     field_gain,
     readout,
-    site_result,
-    response,
+    both,
     packet,
     everyone,
     near_rows,
@@ -62,10 +61,10 @@
     extra_cols,
     rim_out,
     rim_in,
-    index_rows,
     geometry,
     hot,
     third,
+    edge_weight,
     wide_in,
     wide_mid,
     wide_out,
@@ -74,6 +73,8 @@
     hidden_ref,
     acc,
     outside,
+    pairs,
+    terms,
     term_out,
     term_in,
     all_send,
@@ -87,10 +88,11 @@
 ):
     g = lax.axis_index("grp")
     p = lax.axis_index("dom") * n_sub + lax.axis_index("sub")
+    site_result, response = both.at[0], both.at[1]
     n = n_dom * n_sub
     rows = positions.shape[1]
     own_blocks = rows // BLOCK
-    slots = neighbours.shape[1]
+    slots = neighbours.shape[0]
     listed = blocks.shape[0]
     layers, basis, radial = radial_in.shape
     channels = features.shape[1]
@@ -222,56 +224,7 @@
     def _(i):
         packet_copy(i).start()
 
-    wide = jnp.concatenate(
-        [neighbours[...].astype(F32), jnp.zeros((rows, BLOCK - slots), F32)], axis=1
-    )
-    index_rows[...] = wide.T[:slots, :].astype(jnp.int32)
     own_cols[...] = own.T
-
-    @pl.when(g == 0)
-    def _():
-        lane = lax.broadcasted_iota(jnp.int32, (rows, rows + 2 * rim), 1)
-        for k in range(slots):
-            hot[k] = jnp.where(neighbours[:, k : k + 1] == lane, 1.0, 0.0).astype(BF16)
-        spread_r = (
-            lax.broadcasted_iota(jnp.int32, (channels, radial), 0) % radial
-            == lax.broadcasted_iota(jnp.int32, (channels, radial), 1)
-        ).astype(F32).astype(BF16)
-        spread_c = (
-            lax.broadcasted_iota(jnp.int32, (radial, channels), 1) % radial
-            == lax.broadcasted_iota(jnp.int32, (radial, channels), 0)
-        ).astype(F32).astype(BF16)
-        same_in = (
-            lax.broadcasted_iota(jnp.int32, (pack * basis, channels), 0) // basis
-            == lax.broadcasted_iota(jnp.int32, (pack * basis, channels), 1) // radial
-        )
-        same_mid = (
-            lax.broadcasted_iota(jnp.int32, (channels, channels), 0) // radial
-            == lax.broadcasted_iota(jnp.int32, (channels, channels), 1) // radial
-        )
-        for layer in range(layers):
-            flat = jnp.dot(radial_in[layer], spread_c, preferred_element_type=F32)
-            wide_in[layer] = jnp.where(
-                same_in, jnp.concatenate([flat] * pack, axis=0), 0.0
-            ).astype(BF16)
-            for m in range(2):
-                flat = jnp.dot(
-                    jnp.dot(spread_r, radial_mid[layer, m], preferred_element_type=F32).astype(
-                        BF16
-                    ),
-                    spread_c,
-                    preferred_element_type=F32,
-                )
-                wide_mid[layer, m] = jnp.where(same_mid, flat, 0.0).astype(BF16)
-            for j in range(pack):
-                wide_out[layer, j] = jnp.zeros((channels, channels), BF16)
-                wide_out[layer, j, j * radial : (j + 1) * radial, :] = radial_out[layer]
-
-    pltpu.make_async_copy(everyone, everyone, all_recv).wait()
-    for l in range(listed):
-        tile = everyone[blocks[l]]
-        near_rows[:, l * BLOCK : (l + 1) * BLOCK] = tile
-        near_cols[l * BLOCK : (l + 1) * BLOCK, :] = tile.T
 
     def field(targets, source_cols, count, charge, dipole):
         x, y, z = (targets[c : c + 1, :] for c in range(3))
@@ -299,18 +252,14 @@
             )
 
         zero = jnp.zeros((8, width), F32)
-        sums = lax.fori_loop(0, count // 8, step, (zero, zero, zero), unroll=4)
+        sums = lax.fori_loop(0, count // 8, step, (zero, zero, zero), unroll=16)
         return [jnp.sum(s, axis=0, keepdims=True) for s in sums]
-
-    out = field(own, near_cols, listed * BLOCK, lambda at, source: source[:, 3:4], False)
-    for c in range(3):
-        outside[c : c + 1, :] = out[c]
 
     def edges():
         arrive(rim_copy, 0)
         for tile in range(own_blocks):
             at = slice(tile * BLOCK, (tile + 1) * BLOCK)
-            index = index_rows[:, at]
+            index = neighbours[:, at]
             local = index & (BLOCK - 1)
             chunk = lax.shift_right_logical(index, 7)
             picked = []
@@ -331,10 +280,108 @@
                 near_rows[:, half : half + 2 * BLOCK], own_cols, rows, charge, dipole
             )
             for c in range(3):
-                for l in range(2):
-                    term_out[c * listed + half // BLOCK + l] = out[c][
-                        0, l * BLOCK : (l + 1) * BLOCK
-                    ]
+                terms[c : c + 1, half : half + 2 * BLOCK] = out[c]
+
+    centre = lax.broadcasted_iota(jnp.int32, (basis, rows), 0).astype(F32) * SPACING
+
+    def radial_step(q, layer):
+        parts = []
+        for j in range(pack):
+            away = jnp.broadcast_to(geometry[0, pl.ds(q * pack + j, 1), :], (basis, rows))
+            away = away - centre
+            parts.append(jnp.exp(-(away * away)))
+        wave = jnp.concatenate(parts, axis=0).astype(BF16)
+        h = lax.dot_general(
+            wave, wide_in[layer], (((0,), (0,)), ((), ())), preferred_element_type=F32
+        )
+        h = silu(h).astype(BF16)
+        for m in range(2):
+            h = silu(jnp.dot(h, wide_mid[layer, m], preferred_element_type=F32)).astype(BF16)
+        third[layer, q] = h
+
+    def radial_net(layer):
+        @pl.loop(0, groups)
+        def _(q):
+            radial_step(q, layer)
+
+    def edge_net(layer):
+        @pl.loop(0, pack)
+        def _(j):
+            weight = jnp.dot(
+                third[layer].reshape(groups * rows, channels),
+                wide_out[layer, j],
+                preferred_element_type=F32,
+            )
+            edge_weight[j] = weight.reshape(groups, rows, channels)
+
+    @pl.when(g == 0)
+    def _():
+        lane = lax.broadcasted_iota(jnp.int32, (rows, rows + 2 * rim), 1)
+        listing = jnp.concatenate(
+            [neighbours[...].astype(F32), jnp.zeros((BLOCK - slots, rows), F32)], axis=0
+        ).T.astype(jnp.int32)
+        for k in range(slots):
+            hot[k % pack, k // pack] = jnp.where(listing[:, k : k + 1] == lane, 1.0, 0.0).astype(BF16)
+        spread_r = (
+            lax.broadcasted_iota(jnp.int32, (channels, radial), 0) % radial
+            == lax.broadcasted_iota(jnp.int32, (channels, radial), 1)
+        ).astype(F32).astype(BF16)
+        spread_c = (
+            lax.broadcasted_iota(jnp.int32, (radial, channels), 1) % radial
+            == lax.broadcasted_iota(jnp.int32, (radial, channels), 0)
+        ).astype(F32).astype(BF16)
+        same_in = (
+            lax.broadcasted_iota(jnp.int32, (pack * basis, channels), 0) // basis
+            == lax.broadcasted_iota(jnp.int32, (pack * basis, channels), 1) // radial
+        )
+        same_mid = (
+            lax.broadcasted_iota(jnp.int32, (channels, channels), 0) // radial
+            == lax.broadcasted_iota(jnp.int32, (channels, channels), 1) // radial
+        )
+        for layer in range(layers):
+            flat = jnp.dot(radial_in[layer], spread_c, preferred_element_type=F32)
+            wide_in[layer] = jnp.where(
+                same_in, jnp.concatenate([flat] * pack, axis=0), 0.0
+            ).astype(BF16)
+            for m in range(2):
+                flat = jnp.dot(
+                    jnp.dot(spread_r, radial_mid[layer, m], preferred_element_type=F32).astype(
+                        BF16
+                    ),
+                    spread_c,
+                    preferred_element_type=F32,
+                )
+                wide_mid[layer, m] = jnp.where(same_mid, flat, 0.0).astype(BF16)
+            for j in range(pack):
+                wide_out[layer, j] = jnp.zeros((channels, channels), BF16)
+                wide_out[layer, j, j * radial : (j + 1) * radial, :] = radial_out[layer]
+        for at, _, dist_sq, _, _, _ in edges():
+            geometry[0, :, at] = jnp.sqrt(dist_sq)
+        radial_net(0)
+
+    @pl.when(g == 1)
+    def _():
+        for at, offset, dist_sq, source_charge, _, _ in edges():
+            w = lax.rsqrt(dist_sq)
+            w2 = w * w
+            w3 = w2 * w
+            s = source_charge * w3
+            for c in range(3):
+                geometry[c, :, at] = offset[c]
+                extra = jnp.sum(offset[c] * s, axis=0, keepdims=True)
+                pairs[c : c + 1, at] = extra
+            geometry[3, :, at] = w3
+            geometry[4, :, at] = 3.0 * (w3 * w2)
+
+    pltpu.make_async_copy(everyone, everyone, all_recv).wait()
+    for l in range(listed):
+        tile = everyone[blocks[l]]
+        near_rows[:, l * BLOCK : (l + 1) * BLOCK] = tile
+        near_cols[l * BLOCK : (l + 1) * BLOCK, :] = tile.T
+
+    out = field(own, near_cols, listed * BLOCK, lambda at, source: source[:, 3:4], False)
+    for c in range(3):
+        outside[c : c + 1, :] = out[c]
 
     @pl.when(g == 0)
     def _():
@@ -357,77 +404,43 @@
             start(lift_copy, layer)
             tables[layer, 0:rows] = lifted
 
-        lift(0)
-        for at, _, dist_sq, _, _, _ in edges():
-            geometry[0, :, at] = jnp.sqrt(dist_sq)
-
-        centre = lax.broadcasted_iota(jnp.int32, (basis, rows), 0).astype(F32) * SPACING
-
-        def radial_step(q, layer):
-            parts = []
-            for j in range(pack):
-                away = jnp.broadcast_to(geometry[0, pl.ds(q * pack + j, 1), :], (basis, rows))
-                away = away - centre
-                parts.append(jnp.exp(-(away * away)))
-            wave = jnp.concatenate(parts, axis=0).astype(BF16)
-            h = lax.dot_general(
-                wave, wide_in[layer], (((0,), (0,)), ((), ())), preferred_element_type=F32
-            )
-            h = silu(h).astype(BF16)
-            for m in range(2):
-                h = silu(jnp.dot(h, wide_mid[layer, m], preferred_element_type=F32)).astype(BF16)
-            third[layer, q] = h
-
         for layer in range(layers):
-
-            @pl.loop(0, groups)
-            def _(q):
-                radial_step(q, layer)
-
-        for layer in range(layers):
-            if layer:
-                lift(layer)
+            lift(layer)
+            edge_net(layer)
+            if layer + 1 < layers:
+                radial_net(layer + 1)
             arrive(lift_copy, layer)
             acc[...] = jnp.zeros_like(acc)
 
-            @pl.loop(0, groups)
-            def _(q):
-                h = third[layer, q]
-                table = tables[layer]
-                total = None
-                for j in range(pack):
-                    edge_weight = jnp.dot(h, wide_out[layer, j], preferred_element_type=F32)
-                    source = jnp.dot(hot[q * pack + j], table, preferred_element_type=F32)
-                    part = edge_weight * source
-                    total = part if total is None else total + part
-                acc[...] += total
+            @pl.loop(0, pack)
+            def _(j):
+                source = jnp.dot(
+                    hot[j].reshape(groups * rows, rows + 2 * rim),
+                    tables[layer],
+                    preferred_element_type=F32,
+                )
+                product = edge_weight[j] * source.reshape(groups, rows, channels)
+                acc[...] += jnp.sum(product, axis=0)
 
             message = (acc[...] * (1.0 / slots)).astype(BF16)
             update = silu(jnp.dot(message, node_out[layer], preferred_element_type=F32))
             hidden_ref[...] = (hidden_ref[...].astype(F32) + update).astype(BF16)
 
-        readouts = jnp.dot(hidden_ref[...], readout[...], preferred_element_type=F32)
-        extra_cols[:, 0:2] = readouts
-        padded = jnp.concatenate([readouts, jnp.zeros((rows, BLOCK - 2), F32)], axis=1)
-        site_result[0:2, :] = padded.T[0:2, :]
+        across = (((1,), (1,)), ((), ()))
+        extra_cols[:, 0:2] = lax.dot_general(
+            hidden_ref[...], readout[...], across, preferred_element_type=F32
+        )
+        site_result[0:2, :] = lax.dot_general(
+            readout[...], hidden_ref[...], across, preferred_element_type=F32
+        )
         send_terms(lambda at, source: extra_cols[at, 0:1], False)
         for layer in range(layers):
             gone(lift_copy, layer)
 
     @pl.when(g == 1)
     def _():
-        for at, offset, dist_sq, source_charge, _, _ in edges():
-            w = lax.rsqrt(dist_sq)
-            w2 = w * w
-            w3 = w2 * w
-            s = source_charge * w3
-            for c in range(3):
-                geometry[c, :, at] = offset[c]
-                extra = jnp.sum(offset[c] * s, axis=0, keepdims=True)
-                outside[c : c + 1, at] = outside[c : c + 1, at] + extra
-            geometry[3, :, at] = w3
-            geometry[4, :, at] = 3.0 * (w3 * w2)
         gain = polar[...]
+        outside[...] = outside[...] + pairs[...]
         dipole = [gain * outside[c : c + 1, :] for c in range(3)]
         for sweep in range(SWEEPS):
             step = 1 + sweep
@@ -438,7 +451,7 @@
             fresh = [[], [], []]
             for tile in range(own_blocks):
                 at = slice(tile * BLOCK, (tile + 1) * BLOCK)
-                index = index_rows[:, at]
+                index = neighbours[:, at]
                 local = index & (BLOCK - 1)
                 chunk = lax.shift_right_logical(index, 7)
                 d = []
@@ -464,12 +477,19 @@
         for sweep in range(SWEEPS):
             gone(rim_copy, 1 + sweep)
 
-    for l in range(listed):
-        term_out[3 * listed + l] = jnp.full((BLOCK,), blocks[l].astype(F32), F32)
+    @pl.loop(0, n)
+    def _(q):
+        for b in range(own_blocks):
+            total = jnp.zeros((3, BLOCK), F32)
+            for l in range(listed):
+                total = total + jnp.where(
+                    blocks[l] == q * own_blocks + b, terms[:, l * BLOCK : (l + 1) * BLOCK], 0.0
+                )
+            term_out[q, b * 3 : (b + 1) * 3, :] = total
 
     def term_copy(i):
         return pltpu.make_async_remote_copy(
-            src_ref=term_out,
+            src_ref=term_out.at[peer(i)],
             dst_ref=term_in.at[p],
             send_sem=term_send,
             recv_sem=term_recv,
@@ -485,27 +505,9 @@
     pltpu.make_async_copy(everyone, everyone, all_send).wait()
     pltpu.make_async_copy(term_in, term_in, term_recv).wait()
 
-    zero = tuple(jnp.zeros((listed, BLOCK), F32) for _ in range(3 * own_blocks))
-
-    def collect(i, sums):
-        terms = term_in[i]
-        ids = terms[3 * listed :, :]
-        fresh = []
-        for b in range(own_blocks):
-            mine = (p * own_blocks + b).astype(F32) == ids
-            for c in range(3):
-                fresh.append(
-                    sums[b * 3 + c]
-                    + jnp.where(mine, terms[c * listed : (c + 1) * listed, :], 0.0)
-                )
-        return tuple(fresh)
-
-    sums = lax.fori_loop(0, n, collect, zero)
+    total = jnp.sum(term_in[...], axis=0)
     for b in range(own_blocks):
-        for c in range(3):
-            response[c : c + 1, b * BLOCK : (b + 1) * BLOCK] = jnp.sum(
-                sums[b * 3 + c], axis=0, keepdims=True
-            )
+        response[:, b * BLOCK : (b + 1) * BLOCK] = total[b * 3 : (b + 1) * 3, :]
     pltpu.make_async_copy(term_in, term_in, term_send).wait()
 
 
@@ -539,14 +541,11 @@
     specs = [vmem] * 14
     specs[6] = pl.BlockSpec(memory_space=pltpu.SMEM)
     dma = pltpu.SemaphoreType.DMA
-    return pl.pallas_call(
+    both = pl.pallas_call(
         functools.partial(kernel, n_dom, n_sub),
-        out_shape=(
-            jax.ShapeDtypeStruct((3, rows), F32),
-            jax.ShapeDtypeStruct((3, rows), F32),
-        ),
+        out_shape=jax.ShapeDtypeStruct((2, 3, rows), F32),
         in_specs=specs,
-        out_specs=(vmem, vmem),
+        out_specs=vmem,
         scratch_shapes=[
             pltpu.VMEM((own_blocks, 8, BLOCK), F32),
             pltpu.VMEM((n * own_blocks, 8, BLOCK), F32),
@@ -557,10 +556,10 @@
             pltpu.VMEM((rows, 8), F32),
             pltpu.VMEM((1 + SWEEPS, 2, 8, rim), F32),
             pltpu.VMEM((1 + SWEEPS, 2, 8, rim), F32),
-            pltpu.VMEM((slots, rows), jnp.int32),
             pltpu.VMEM((5, slots, rows), F32),
-            pltpu.VMEM((slots, rows, rows + 2 * rim), BF16),
+            pltpu.VMEM((pack, slots // pack, rows, rows + 2 * rim), BF16),
             pltpu.VMEM((layers, slots // pack, rows, channels), BF16),
+            pltpu.VMEM((pack, slots // pack, rows, channels), F32),
             pltpu.VMEM((layers, pack * basis, channels), BF16),
             pltpu.VMEM((layers, 2, channels, channels), BF16),
             pltpu.VMEM((layers, pack, channels, channels), BF16),
@@ -569,8 +568,10 @@
             pltpu.VMEM((rows, channels), BF16),
             pltpu.VMEM((rows, channels), F32),
             pltpu.VMEM((3, rows), F32),
-            pltpu.VMEM((4 * listed, BLOCK), F32),
-            pltpu.VMEM((n, 4 * listed, BLOCK), F32),
+            pltpu.VMEM((3, rows), F32),
+            pltpu.VMEM((3, listed * BLOCK), F32),
+            pltpu.VMEM((n, own_blocks * 3, BLOCK), F32),
+            pltpu.VMEM((n, own_blocks * 3, BLOCK), F32),
             dma(()),
             dma(()),
             dma((1 + SWEEPS, 2)),
@@ -588,7 +589,7 @@
         charges.reshape(1, -1),
         polar.reshape(1, -1),
         features,
-        neighbours,
+        neighbours.T,
         send_rows,
         blocks,
         radial_in,
@@ -597,8 +598,9 @@
         node_in,
         node_out,
         field_gain.reshape(1, -1),
-        readout,
+        readout.T,
     )
+    return both[0], both[1]
 
 
 def solution(mesh):

time: 50.7 us -> 40.4 us (0.80)
  Pallas kernels: 45.7 us -> 38.3 us
  local copies, waits for them, and re-layouts: 4.04 us -> 1.28 us
    pallas_call x1, Pallas kernels: 45.7 us -> 38.3 us  [local(): pl.pallas_call(functools.partial(kernel, n_dom, n_sub), out_shape=jax.Sha...]
    unnamed x10 -> x0, local copies, waits for them, and re-layouts: 4.04 us -> none
    squeeze x0 -> x1, local copies, waits for them, and re-layouts: none -> 1.28 us  [local(): return (both[0], both[1])]
where the time goes in v2:
time: 40.4 us; the launch traced here: 40.2 us
  Pallas kernels  38.3 us (95%)
  local copies, waits for them, and re-layouts  1.28 us (3%)
  between operations  0.64 us (2%)
    pallas_call x1, Pallas kernels, local(): pl.pallas_call(functools.partial(kernel, n_dom, n_sub), out_shape=jax.Sha...  38.3 us
    squeeze x1, local copies, waits for them, and re-layouts, local(): return (both[0], both[1])  1.28 us

profile of v2, /device:TPU:1, one launch (start us, length us, event | category | flops | bytes accessed | tf_op | source)
XLA Modules:
  0.0 40.2 jit_solution(7850003339943359929)
XLA Ops:
  0.6 38.3 %shard_map.149 = f32[2,3,256]{2,1,0:T(4,128)} custom-call(f32[3,256]{1,0:T(4,128)} %positions.1, f32[1,256]{1,0:T(1,128)} %bitcast.10, f32[1,256]{1,0:T(1,128)} %bitcast.11, bf16[256,256]{1,0:T(8,128)(2,1)} %features.1, s32[32,256]{1,0:T(8,128)} %bitcast.9, s32[2,128]{1,0:T(2,128)} %send_rows.1, s32[4]{0:T(128)} %blocks.1, bf16[2,8,64]{2,1,0:T(8,128)(2,1)} %radial_in.1, ...), custom_call_target="tpu_custom_call" | custom-call | tf_op jit(solution)/shard_map/pallas_call | solution.py:544
  38.9 1.3 %slice_bitcast_fusion = (f32[3,256]{1,0:T(4,128)}, f32[3,256]{1,0:T(4,128)}) fusion(f32[2,3,256]{2,1,0:T(4,128)} %shard_map.149), kind=kLoop, calls=%fused_computation | loop fusion | bytes 12288 | tf_op jit(solution)/shard_map/squeeze | solution.py:603

commit v3 on v2

--- a/solution.py
+++ b/solution.py
@@ -300,7 +300,7 @@
         third[layer, q] = h
 
     def radial_net(layer):
-        @pl.loop(0, groups)
+        @pl.loop(0, groups, unroll=4)
         def _(q):
             radial_step(q, layer)
 
@@ -412,7 +412,7 @@
             arrive(lift_copy, layer)
             acc[...] = jnp.zeros_like(acc)
 
-            @pl.loop(0, pack)
+            @pl.loop(0, pack, unroll=2)
             def _(j):
                 source = jnp.dot(
                     hot[j].reshape(groups * rows, rows + 2 * rim),

time: 40.4 us -> 37 us (0.916)
  Pallas kernels: 38.3 us -> 34.9 us
    pallas_call x1, Pallas kernels: 38.3 us -> 34.9 us  [local(): pl.pallas_call(functools.partial(kernel, n_dom, n_sub), out_shape=jax.Sha...]
where the time goes in v3:
time: 37 us; the launch traced here: 36.8 us
  Pallas kernels  34.9 us (94%)
  local copies, waits for them, and re-layouts  1.28 us (3%)
  between operations  0.64 us (2%)
    pallas_call x1, Pallas kernels, local(): pl.pallas_call(functools.partial(kernel, n_dom, n_sub), out_shape=jax.Sha...  34.9 us
    squeeze x1, local copies, waits for them, and re-layouts, local(): return (both[0], both[1])  1.28 us

profile of v3, /device:TPU:1, one launch (start us, length us, event | category | flops | bytes accessed | tf_op | source)
XLA Modules:
  0.0 36.8 jit_solution(8033037425525942304)
XLA Ops:
  0.6 34.9 %shard_map.149 = f32[2,3,256]{2,1,0:T(4,128)} custom-call(f32[3,256]{1,0:T(4,128)} %positions.1, f32[1,256]{1,0:T(1,128)} %bitcast.10, f32[1,256]{1,0:T(1,128)} %bitcast.11, bf16[256,256]{1,0:T(8,128)(2,1)} %features.1, s32[32,256]{1,0:T(8,128)} %bitcast.9, s32[2,128]{1,0:T(2,128)} %send_rows.1, s32[4]{0:T(128)} %blocks.1, bf16[2,8,64]{2,1,0:T(8,128)(2,1)} %radial_in.1, ...), custom_call_target="tpu_custom_call" | custom-call | tf_op jit(solution)/shard_map/pallas_call | solution.py:544
  35.5 1.3 %slice_bitcast_fusion = (f32[3,256]{1,0:T(4,128)}, f32[3,256]{1,0:T(4,128)}) fusion(f32[2,3,256]{2,1,0:T(4,128)} %shard_map.149), kind=kLoop, calls=%fused_computation | loop fusion | bytes 12288 | tf_op jit(solution)/shard_map/squeeze | solution.py:603
